TPU v7x, 32 devices: a whole 2x2x4 slice. The times are simulated.
32 devices in a mesh: grp: 2 (over x), slab: 16 (over z, y, core).
Axes of the slice: x: 2, y: 2, z: 4, core: 2. Of those that a mesh axis runs over, the one named last changes fastest.
Arguments:
- estimate: float32 [2, 8, 4, 48, 32], P(None, None, 'grp', 'slab'), parts along dimension 2, may hold values from -6 to 6
- measured: float32 [2, 8, 4, 48, 32], P(None, None, 'grp', 'slab'), parts along dimension 2, may hold values from -6 to 6
- sampled_lines: int32 [4, 12], P('grp'), parts along dimension 0, may hold values from 0 to 47, as said below
Outputs:
- updated: float32 [2, 8, 4, 48, 32], P(None, None, 'grp', 'slab'), parts along dimension 2
There are 2 independent parts, one for each index of `grp`. A program takes and returns all parts, laid end to end along the dimension named above; each array names one. Nothing has to cross between parts.
Inputs may be any that keep to these rules, and one draw needn't show every extreme that they name: `sampled_lines`: lines within a frame are distinct, and every frame contains line 48 // 2.
All inputs are finite; a program needn't handle non-finite values.
Results may differ from a plain program's by a relative error of at most 0.0001.
Values sent between devices are 32-bit elements; how exact they have to be, the bound alone decides.
A program may use at most 64 MiB of HBM per device.

v0:
```python
import functools

import jax
import jax.numpy as jnp
from jax import lax
from jax.experimental import pallas as pl
from jax.experimental.pallas import tpu as pltpu
from jax.sharding import PartitionSpec as P

LANES = 128


def gather_kernel(n, x_ref, out_ref, send_sem, recv_sem, own_sem):
    me = lax.axis_index("slab")

    def greet(k, carry):
        pl.semaphore_signal(
            pltpu.get_barrier_semaphore(), inc=1, device_id={"slab": lax.rem(me + k, n)}
        )
        return carry

    lax.fori_loop(1, n, greet, 0)
    own = pltpu.make_async_copy(x_ref, out_ref.at[me], own_sem)
    own.start()
    pl.semaphore_wait(pltpu.get_barrier_semaphore(), n - 1)

    def copy(k, place):
        return pltpu.make_async_remote_copy(
            src_ref=x_ref,
            dst_ref=out_ref.at[place],
            send_sem=send_sem.at[k - 1],
            recv_sem=recv_sem.at[k - 1],
            device_id={"slab": lax.rem(me + k, n)},
        )

    def send(k, carry):
        copy(k, me).start()
        return carry

    def receive(k, carry):
        copy(k, lax.rem(me + n - k, n)).wait_recv()
        return carry

    def finish(k, carry):
        copy(k, me).wait_send()
        return carry

    lax.fori_loop(1, n, send, 0)
    own.wait()
    lax.fori_loop(1, n, receive, 0)
    lax.fori_loop(1, n, finish, 0)


def whole_kernel(n, sizes, x_ref, out_ref, all_ref, send_sem, recv_sem, own_sem, *scratch):
    gather_kernel(n, x_ref, all_ref, send_sem, recv_sem, own_sem)
    filter_kernel(n, *sizes, all_ref, out_ref, *scratch)


def couplings(frames):
    table = {}
    for s in range(frames):
        for s2 in range(frames):
            for d in range(1 - frames, frames):
                if 0 <= s + d < frames and 0 <= s2 + d < frames:
                    n = sum(
                        1
                        for t in range(frames)
                        if 0 <= t + d < frames and abs(s - t) <= 2 and abs(s2 - t) <= 2
                    )
                    if n:
                        table[s, s2, d] = n
    return table


def halves(x):
    hi = x.astype(jnp.bfloat16)
    return hi, (x - hi.astype(jnp.float32)).astype(jnp.bfloat16)


def dot_nt(a, b):
    return lax.dot_general(a, b, (((1,), (1,)), ((), ())), preferred_element_type=jnp.float32)


def dot_nn(a, b):
    return lax.dot_general(a, b, (((1,), (0,)), ((), ())), preferred_element_type=jnp.float32)


def filter_kernel(n, frames, coils, rows, readout, all_ref, out_ref, *scratch):
    q_hi, q_lo, l_hi, l_lo, p_hi, p_lo, m_hi, m_lo = scratch
    me = lax.axis_index("slab")
    stride = readout + 4
    fit = LANES // stride
    channels = 2 * frames * coils
    size = 5 * channels
    total = n * rows
    deep = -(-total // fit)
    near = -(-(rows + 4) // fit)
    lane = lax.broadcasted_iota(jnp.int32, (1, LANES), 1)
    slot = lane // stride
    valid = (lane % stride < readout) & (slot < fit)

    def tile(lines):
        result = jnp.zeros((channels, LANES), jnp.float32)
        for g, source in enumerate(lines):
            if source is not None:
                block, j = source
                by = (g - j) * stride % LANES
                moved = pltpu.roll(block, by, 1) if by else block
                result = jnp.where(slot == g, moved, result)
        return result

    def spread(cells):
        moved = [pltpu.roll(cells, LANES - e, 1) if e else cells for e in range(5)]
        return jnp.concatenate(
            [
                moved[e][g * coils : (g + 1) * coils]
                for g in range(2 * frames)
                for e in range(5)
            ],
            axis=0,
        )

    for k in range(deep + 4):
        lines = []
        for g in range(fit):
            line = k + deep * g
            lines.append((all_ref[line // rows], line % rows) if line < total else None)
        hi, lo = halves(spread(tile(lines)))
        at = pl.ds(k * LANES, LANES)
        q_hi[:, at] = hi
        q_lo[:, at] = lo
        if k < deep:
            l_hi[:, at] = jnp.where(valid, hi, jnp.zeros_like(hi))
            l_lo[:, at] = jnp.where(valid, lo, jnp.zeros_like(lo))

    for k in range(near + 4):
        lines = []
        for g in range(fit):
            line = k + near * g - 4
            other = me + line // rows
            block = all_ref[jnp.clip(other, 0, n - 1)]
            lines.append((jnp.where((other >= 0) & (other < n), block, 0.0), line % rows))
        hi, lo = halves(spread(tile(lines)))
        p_hi[:, pl.ds(k * LANES, LANES)] = hi
        p_lo[:, pl.ds(k * LANES, LANES)] = lo

    def gram(first, count, dy):
        left = pl.ds(first * LANES, count * LANES)
        right = pl.ds((first + dy) * LANES, count * LANES)
        return (
            dot_nt(q_hi[:, right], l_hi[:, left])
            + dot_nt(q_hi[:, right], l_lo[:, left])
            + dot_nt(q_lo[:, right], l_hi[:, left])
        )

    def line_gram(line, dy):
        left = pl.ds(line % deep * LANES, LANES)
        right = pl.ds((line % deep + dy) * LANES, LANES)
        pick = slot == line // deep
        hi = jnp.where(pick, l_hi[:, left], 0)
        lo = jnp.where(pick, l_lo[:, left], 0)
        return dot_nt(q_hi[:, right], hi) + dot_nt(q_hi[:, right], lo) + dot_nt(q_lo[:, right], hi)

    step = 16
    sums = []
    for dy in range(5):
        sofar = None
        for first in range(0, deep, step):
            term = gram(first, min(step, deep - first), dy)
            sofar = term if sofar is None else sofar + term
        sums.append(sofar)

    zero0 = [None, None, sums[0]]
    zero0[1] = sums[0] - line_gram(total - 1, 0)
    zero0[0] = zero0[1] - line_gram(total - 2, 0)
    zero0.append(sums[0] - line_gram(0, 0))
    zero0.append(zero0[3] - line_gram(1, 0))
    one = [sums[1] - line_gram(total - 2, 1), sums[1], sums[1], sums[1] - line_gram(0, 1)]

    row_i = lax.broadcasted_iota(jnp.int32, (size, size), 0)
    col_i = lax.broadcasted_iota(jnp.int32, (size, size), 1)
    per_frame = size // (2 * frames)
    row_frame = row_i // per_frame % frames
    col_frame = col_i // per_frame % frames
    col_part = col_i // (size // 2)
    weight = jnp.zeros((size, size), jnp.float32)
    for s in range(frames):
        reach = sum(1 for t in range(frames) if abs(s - t) <= 2)
        weight = jnp.where(row_frame == s, float(reach), weight)
    diagonal = zero0[0] + zero0[1] + zero0[2] + zero0[3] + zero0[4]
    diagonal = jnp.where(row_i == col_i, diagonal * weight, 0.0)
    trace = jnp.sum(jnp.sum(diagonal, axis=0, keepdims=True), axis=1, keepdims=True)
    scale = trace / (125 * coils) + 1e-06

    table = couplings(frames)
    half = size // 2

    def lane_roll(x, by):
        by = by % size
        return x if by == 0 else jnp.concatenate([x[:, size - by :], x[:, : size - by]], axis=1)

    def mixed(raw):
        swapped = lane_roll(raw, half)
        sign = jnp.where(col_part[:half] == 0, 1.0, -1.0)
        whole = jnp.concatenate(
            [raw[:half] + sign * swapped[half:], raw[half:] - sign * swapped[:half]], axis=0
        )
        result = jnp.zeros_like(whole)
        for d in range(1 - frames, frames):
            terms = {k: v for k, v in table.items() if k[2] == d}
            if not terms:
                continue
            by = d * per_frame
            moved = lane_roll(whole, -by)
            if by % size:
                moved = jnp.concatenate([moved[by % size :], moved[: by % size]], axis=0)
            factor = jnp.zeros_like(whole)
            for (s, s2, _), v in terms.items():
                factor = jnp.where((row_frame == s) & (col_frame == s2), float(v), factor)
            result = result + factor * moved
        return result

    def put(row, col, x):
        hi, lo = halves(x)
        m_hi[col, pl.ds(row * size, size), :] = hi
        m_lo[col, pl.ds(row * size, size), :] = lo

    for b in range(5):
        put(b, b, mixed(zero0[b]))
    kept = None
    for b in range(4):
        if b != 2:
            kept = mixed(one[b])
            turned = kept.T
        put(b + 1, b, kept)
        put(b, b + 1, turned)
    for dy in range(2, 5):
        kept = mixed(sums[dy])
        turned = kept.T
        for b in range(5 - dy):
            put(b + dy, b, kept)
            put(b, b + dy, turned)

    wide = near * LANES
    cell = lax.broadcasted_iota(jnp.int32, (1, wide), 1)
    cell_slot = cell % LANES // stride
    line = cell // LANES + near * cell_slot
    usable = (cell % LANES % stride < readout) & (cell_slot < fit) & (line < rows + 4)
    line = line + me * rows - 2
    usable = usable & (line >= 0) & (line < total)
    gathers = {}
    for b2 in range(5):
        at = pl.ds(b2 * size, size)
        piece = jnp.zeros((size, wide), jnp.float32)
        for b in range(5):
            cols = pl.ds(b * LANES, wide)
            piece = piece + (
                dot_nn(m_hi[b, at, :], p_hi[:, cols])
                + dot_nn(m_hi[b, at, :], p_lo[:, cols])
                + dot_nn(m_lo[b, at, :], p_hi[:, cols])
            )
        piece = jnp.where(usable, piece, 0.0)
        for e in range(5):
            part = jnp.concatenate(
                [
                    piece[(g * 5 + e) * coils : (g * 5 + e + 1) * coils]
                    for g in range(2 * frames)
                ],
                axis=0,
            )
            for j in range(rows):
                line = j - b2 + 4
                k, g = line % near, line // near
                term = jnp.where(slot == g, part[:, k * LANES : (k + 1) * LANES], 0.0)
                key = (e, j - g)
                gathers[key] = gathers[key] + term if key in gathers else term
    folded = jnp.zeros((channels, LANES), jnp.float32)
    for (e, moves), term in gathers.items():
        by = (moves * stride + e - 2) % LANES
        folded = folded + (pltpu.roll(term, by, 1) if by else term)
    out_ref[...] = folded / (125.0 * scale)


def local(estimate, measured, sampled_lines):
    _, coils, frames, rows, readout = estimate.shape
    n = lax.axis_size("slab")
    place = lax.axis_index("slab")
    stride = readout + 4
    channels = 2 * frames * coils
    size = 5 * channels
    cells = jnp.transpose(estimate, (0, 2, 1, 3, 4)).reshape(channels, rows, readout)
    cells = jnp.pad(cells, ((0, 0), (0, 0), (2, 2))).reshape(channels, rows * stride)
    block = jnp.pad(cells, ((0, 0), (0, LANES - rows * stride)))
    fit = LANES // stride
    deep = -(-n * rows // fit) * LANES
    near = -(-(rows + 4) // fit) * LANES
    bf16 = jnp.bfloat16
    folded = pl.pallas_call(
        functools.partial(whole_kernel, n, (frames, coils, rows, readout)),
        out_shape=jax.ShapeDtypeStruct((channels, LANES), jnp.float32),
        in_specs=[pl.BlockSpec(memory_space=pltpu.VMEM)],
        out_specs=pl.BlockSpec(memory_space=pltpu.VMEM),
        scratch_shapes=[
            pltpu.VMEM((n, channels, LANES), jnp.float32),
            pltpu.SemaphoreType.DMA((n,)),
            pltpu.SemaphoreType.DMA((n,)),
            pltpu.SemaphoreType.DMA,
            pltpu.VMEM((size, deep + 4 * LANES), bf16),
            pltpu.VMEM((size, deep + 4 * LANES), bf16),
            pltpu.VMEM((size, deep), bf16),
            pltpu.VMEM((size, deep), bf16),
            pltpu.VMEM((size, near + 4 * LANES), bf16),
            pltpu.VMEM((size, near + 4 * LANES), bf16),
            pltpu.VMEM((5, 5 * size, size), bf16),
            pltpu.VMEM((5, 5 * size, size), bf16),
        ],
        compiler_params=pltpu.CompilerParams(
            vmem_limit_bytes=48 * 1024 * 1024, collective_id=0, has_side_effects=True
        ),
    )(block)
    folded = folded[:, : rows * stride].reshape(2, frames, coils, rows, stride)[..., :readout]
    folded = jnp.transpose(folded, (0, 2, 1, 3, 4))
    line_index = place * rows + jnp.arange(rows, dtype=jnp.int32)
    hit = jnp.any(sampled_lines[:, :, None] == line_index[None, None, :], axis=1)
    return jnp.where(hit[None, None, :, :, None], measured, folded)


def solution(mesh):
    placed = (
        P(None, None, "grp", "slab", None),
        P(None, None, "grp", "slab", None),
        P("grp", None),
    )
    return jax.shard_map(
        local,
        mesh=mesh,
        in_specs=placed,
        out_specs=P(None, None, "grp", "slab", None),
        check_vma=False,
    )
```

profile of v0, /device:TPU:0, one launch (start us, length us, event | category | flops | bytes accessed | tf_op | source)
XLA Modules:
  0.0 22.6 jit_solution(764653630526044569)
XLA Ops:
  0.0 0.0 copy-start.1
  0.0 0.7 %copy-done.1 = s32[2,12]{1,0:T(2,128)S(1)} copy-done((s32[2,12]{1,0:T(2,128)S(1)}, s32[2,12]{1,0:T(2,128)}, u32[]{:S(2)}) %copy-start.1) | copy-done | bytes 120
  0.7 0.2 compare_reduce_fusion
  0.9 0.8 %copy.9 = f32[2,8,2,3,32]{4,1,2,0,3:T(8,128)S(1)} copy(f32[2,8,2,3,32]{4,2,3,1,0:T(2,128)} %param.3) | data formatting | bytes 24576 | tf_op args[0]
  1.7 0.1 pad.8.clone
  1.8 0.1 reshape.16
  1.9 19.1 %shard_map.37 = f32[32,128]{1,0:T(8,128)S(1)} custom-call(f32[32,128]{1,0:T(8,128)S(1)} %pad.9.x_ref), custom_call_target="tpu_custom_call" | custom-call | tf_op jit(solution)/shard_map/pallas_call | solution.py:298
  21.0 0.0 copy-start
  21.0 0.1 reshape.17
  21.1 0.7 %copy-done = f32[2,8,2,3,32]{4,2,3,1,0:T(2,128)S(1)} copy-done((f32[2,8,2,3,32]{4,2,3,1,0:T(2,128)S(1)}, f32[2,8,2,3,32]{4,2,3,1,0:T(2,128)}, u32[]{:S(2)}) %copy-start) | copy-done | bytes 12312
  21.8 0.1 fusion
  21.9 0.7 %copy.12 = f32[2,8,2,3,32]{4,2,3,1,0:T(2,128)} copy(f32[2,8,2,3,32]{4,3,1,2,0:T(4,128)S(1)} %fusion) | data formatting | bytes 24576 | tf_op jit(solution)/shard_map/jit(_where)/select_n | solution.py:325
  (3 shorter events, 0.0 us)
Async XLA Ops:
  0.0 0.7 %copy-start.1 = (s32[2,12]{1,0:T(2,128)S(1)}, s32[2,12]{1,0:T(2,128)}, u32[]{:S(2)}) copy-start(s32[2,12]{1,0:T(2,128)} %param.5) | copy-start | bytes 292
  21.0 0.8 %copy-start = (f32[2,8,2,3,32]{4,2,3,1,0:T(2,128)S(1)}, f32[2,8,2,3,32]{4,2,3,1,0:T(2,128)}, u32[]{:S(2)}) copy-start(f32[2,8,2,3,32]{4,2,3,1,0:T(2,128)} %param.4) | copy-start | bytes 36868
where the time goes:
time: 22.8 us; the launch traced here: 22.6 us
  Pallas kernels  19.1 us (84%)
  local copies, waits for them, and re-layouts  3.15 us (14%)
  other arithmetic  0.27 us (1%)
    pallas_call x1, Pallas kernels, local(): pl.pallas_call(functools.partial(whole_kernel, n, (frames, coils, rows, r...  19.1 us
    unnamed x6, local copies, waits for them, and re-layouts  2.21 us
    select_n x1, local copies, waits for them, and re-layouts, local(): return jnp.where(hit[None, None, :, :, None], measured, folded)  0.66 us

commit v1 on v0

v1 whole, which is shorter than its diff:
```python
import functools

import jax
import jax.numpy as jnp
from jax import lax
from jax.experimental import pallas as pl
from jax.experimental.pallas import tpu as pltpu
from jax.sharding import PartitionSpec as P

LANES = 128
REACH = 4
CHUNK = 24


def couplings(frames):
    table = {}
    for s in range(frames):
        for s2 in range(frames):
            for d in range(1 - frames, frames):
                if 0 <= s + d < frames and 0 <= s2 + d < frames:
                    table[s, s2, d] = sum(
                        1
                        for t in range(frames)
                        if 0 <= t + d < frames and abs(s - t) <= 2 and abs(s2 - t) <= 2
                    )
    return {k: v for k, v in table.items() if v}


def split(x):
    hi = x.astype(jnp.bfloat16).astype(jnp.float32)
    return hi, x - hi


def dot_nt(a, b):
    return lax.dot_general(a, b, (((1,), (1,)), ((), ())), preferred_element_type=jnp.float32)


def dot_nn(a, b):
    return lax.dot_general(a, b, (((1,), (0,)), ((), ())), preferred_element_type=jnp.float32)


def as_bf16(pieces):
    return jnp.concatenate(pieces, axis=0).astype(jnp.bfloat16)


def kernel(
    n, sizes, est_hbm, meas_hbm, picks_hbm, out_ref,
    est, meas, picks, all_ref, left, r_hi, r_lo, weights, p_hi, p_lo, sums, edges,
    send_sem, recv_sem, in_sem,
):
    parts, frames, coils, rows, readout = sizes
    me = lax.axis_index("slab")
    total = n * rows
    deep = total // 2
    chunk = max(d for d in range(1, CHUNK + 1) if deep % d == 0)
    ext = coils * 5
    wide = frames * ext

    loads = [
        pltpu.make_async_copy(est_hbm, est, in_sem.at[0]),
        pltpu.make_async_copy(meas_hbm, meas, in_sem.at[1]),
        pltpu.make_async_copy(picks_hbm, picks, in_sem.at[2]),
    ]
    for copy in loads:
        copy.start()

    def greet(k, carry):
        pl.semaphore_signal(
            pltpu.get_barrier_semaphore(), inc=1, device_id={"slab": lax.rem(me + k, n)}
        )
        return carry

    lax.fori_loop(1, n, greet, 0, unroll=n <= 16)

    def place(line, s, part):
        return pl.ds((part * coils * rows + line) * frames + s, coils, stride=rows * frames)

    loads[0].wait()
    for j in range(rows):
        all_ref[me, j * coils : (j + 1) * coils, :] = jnp.concatenate(
            [est[place(j, s, part), :] for part in range(parts) for s in range(frames)], axis=1
        )
    pl.semaphore_wait(pltpu.get_barrier_semaphore(), n - 1)

    def copy(other, slot):
        return pltpu.make_async_remote_copy(
            src_ref=all_ref.at[slot],
            dst_ref=all_ref.at[slot],
            send_sem=send_sem.at[other],
            recv_sem=recv_sem.at[slot],
            device_id={"slab": other},
        )

    def send(k, carry):
        copy(k + (k >= me).astype(jnp.int32), me).start()
        return carry

    lax.fori_loop(0, n - 1, send, 0, unroll=n <= 16)

    lane = lax.broadcasted_iota(jnp.int32, (1, LANES), 1)
    slot = lane // readout
    x = lane % readout
    second = slot % 2 == 1
    turn = jnp.where(slot < 2, 1.0, -1.0)

    def rolled(v, by):
        by = by % LANES
        return pltpu.roll(v, by, 1) if by else v

    def shifts(v):
        return [
            jnp.where((x + d >= 0) & (x + d < readout), rolled(v, -d), 0.0) if d else v
            for d in range(-2, 3)
        ]

    def halo(d):
        return (me + d >= 0) & (me + d < n)

    near = -(-REACH // rows)
    for d in [s * k for k in range(1, near + 1) for s in (1, -1)]:
        pl.when(halo(d))(lambda d=d: copy(me + d, me + d).wait_recv())

    around = []
    for i in range(rows + 2 * REACH):
        d, j = divmod(i - REACH, rows)
        block = all_ref[jnp.clip(me + d, 0, n - 1), j * coils : (j + 1) * coils, :]
        block = jnp.where(halo(d), block, 0.0) if d else block
        around.append([rolled(block, by * readout) for by in range(LANES // readout)])

    moved = {}
    for dy in range(-REACH, REACH + 1):
        for s in range(frames):
            for part in range(parts):
                v = jnp.zeros((coils, LANES), jnp.float32)
                for j in range(rows):
                    seg = part * frames + s
                    v = jnp.where(slot == j, around[dy + REACH + j][(j - seg) % 4], v)
                moved[dy, s, part] = shifts(v)

    line_at = me * rows + slot

    def coefficient(dy, q=None):
        count = jnp.zeros((1, LANES), jnp.float32)
        for b in range(max(-2, -2 - dy), min(2, 2 - dy) + 1):
            if q is not None and 0 <= q - b < total:
                continue
            count = count + jnp.where((line_at - b >= 0) & (line_at - b < total), 1.0, 0.0)
        return count if q is None else -count

    blocks = [[(dy, None) for dy in range(first, first + 3)] for first in (-4, -1, 2)]
    ends = [
        (0, 0, False, 0, [(0, 0), (1, 0), None]),
        (1, 0, False, 0, [(-1, 1), (0, 1), None]),
        (deep - 1, deep - 2, True, total - 1, [(-1, total - 1), (0, total - 1), None]),
        (deep - 2, deep - 2, True, total - 2, [(0, total - 2), (1, total - 2), None]),
    ]
    blocks += [e[4] for e in ends]
    nothing = jnp.zeros((coils, LANES), jnp.float32)
    tile = frames * LANES
    for t, members in enumerate(blocks):
        for s in range(frames):
            his, los = [[], []], [[], []]
            for member in members:
                factor = None if member is None else coefficient(*member)
                for e in range(5):
                    for part in range(parts):
                        if member is None:
                            hi = lo = nothing
                        else:
                            hi, lo = split(factor * moved[member[0], s, part][e])
                        his[part].append(hi)
                        los[part].append(lo)
            for part in range(parts):
                his[part].append(nothing)
                los[part].append(nothing)
            at = pl.ds(t * tile + s * LANES, LANES)
            bt = pl.ds((len(blocks) + t) * tile + s * LANES, LANES)
            for ref, cells in ((p_hi, his), (p_lo, los)):
                re, im = as_bf16(cells[0]), as_bf16(cells[1])
                ref[at, 0:LANES] = re
                ref[at, LANES : 2 * LANES] = im
                ref[bt, 0:LANES] = -im
                ref[bt, LANES : 2 * LANES] = re

    def arrive(j, carry):
        pl.when(jnp.abs(j - me) > near)(lambda: copy(j, j).wait_recv())
        return carry

    lax.fori_loop(0, n, arrive, 0, unroll=n <= 16)

    def line_block(line):
        if isinstance(line, int):
            if not 0 <= line < total:
                return None
            return all_ref[line // rows, line % rows * coils : (line % rows + 1) * coils, :]
        inside = jnp.clip(line, 0, total - 1)
        block = all_ref[inside // rows, pl.ds(pl.multiple_of(inside % rows * coils, coils), coils), :]
        return jnp.where((line >= 0) & (line < total), block, 0.0)

    def reach_of(line):
        return sum(
            ((line - b >= 0) & (line - b < total)) * jnp.float32(1) for b in range(-2, 3)
        )

    def build(first, energy):
        tiles = {}
        for k in range(-REACH, chunk + REACH):
            lines = [line_block(first + k), line_block(first + k + deep)]
            if 0 <= k < chunk:
                for h in range(2):
                    energy = energy + reach_of(first + k + deep * h) * (lines[h] * lines[h])
            lines = [nothing if v is None else v for v in lines]
            cells = []
            for s in range(frames):
                v = jnp.where(
                    second,
                    rolled(lines[1], (1 - s) * readout),
                    rolled(lines[0], -s * readout),
                )
                cells.append(shifts(v))
            tiles[k] = [[split(v) for v in c] for c in cells]
            if 0 <= k < chunk:
                flat = [p for c in tiles[k] for p in c]
                at = pl.ds(k * LANES, LANES)
                for w in range(2):
                    left[pl.ds(w * 2 * wide, wide), at] = as_bf16([p[w] for p in flat])
                    left[pl.ds(w * 2 * wide + wide, wide), at] = as_bf16(
                        [turn * rolled(p[w], LANES // 2) for p in flat]
                    )
            if k - 2 >= -REACH:
                at = pl.ds((k - 2 + REACH) * LANES, LANES)
                for s in range(frames):
                    for ref, w in ((r_hi, 0), (r_lo, 1)):
                        ref[pl.ds(s * LANES, LANES), at] = as_bf16(
                            [p[w] for m in (k - 2, k - 1, k) for p in tiles[m][s]] + [nothing]
                        )
        return energy

    def product(rows_, right):
        both = dot_nt(rows_, r_hi[:, right])
        rest = dot_nt(rows_[: 2 * wide], r_lo[:, right])
        return both[: 2 * wide] + both[2 * wide :] + rest

    def gram(first):
        return product(left[...], pl.ds((first + REACH) * LANES, chunk * LANES))

    def end(which, base):
        at, start, late, _, _ = ends[which]
        rows_ = left[:, pl.ds((at - base) * LANES, LANES)]
        rows_ = jnp.where(second == late, rows_, jnp.zeros_like(rows_))
        return product(rows_, pl.ds((start - base + REACH) * LANES, LANES))

    energy = nothing
    if chunk == deep:
        energy = build(0, energy)
        found = [gram(m[0][0]) for m in blocks[:3]] + [end(w, 0) for w in range(4)]
    else:
        for t in range(3):
            sums[t] = jnp.zeros((2 * wide, tile), jnp.float32)

        def step(c, energy):
            energy = build(c * chunk, energy)
            for t in range(3):
                sums[t] += gram(blocks[t][0][0])

            @pl.when(c == 0)
            def _():
                for w in range(2):
                    edges[w] = end(w, 0)

            @pl.when(c == deep // chunk - 1)
            def _():
                for w in range(2, 4):
                    edges[w] = end(w, deep - chunk)

            return energy

        energy = lax.fori_loop(0, deep // chunk, step, energy)
        found = [sums[t] for t in range(3)] + [edges[w] for w in range(4)]

    across = sum(jnp.where((x - d >= 0) & (x - d < readout), 1.0, 0.0) for d in range(-2, 3))
    frame = slot % frames
    for s in range(frames):
        reach = sum(1.0 for t in range(frames) if abs(s - t) <= 2)
        across = jnp.where(frame == s, across * reach, across)
    energy = jnp.sum(energy * across, axis=0, keepdims=True)
    scale = jnp.sum(energy, axis=1, keepdims=True) / (125 * coils) + 1e-06

    table = couplings(frames)
    for t, u in enumerate(found):
        for h in range(2):
            for s in range(frames):
                pieces = []
                for s2 in range(frames):
                    total_ = None
                    for d in range(1 - frames, frames):
                        if (s2, s, d) in table:
                            row = h * wide + (s2 + d) * ext
                            term = u[row : row + ext, (s + d) * LANES : (s + d + 1) * LANES]
                            term = float(table[s2, s, d]) * term
                            total_ = term if total_ is None else total_ + term
                    pieces.append(total_)
                hi, lo = split(jnp.concatenate(pieces, axis=0))
                at = pl.ds((h * len(blocks) + t) * tile + s * LANES, LANES)
                weights[0:wide, at] = hi.astype(jnp.bfloat16)
                weights[wide : 2 * wide, at] = lo.astype(jnp.bfloat16)

    both = dot_nn(weights[...], p_hi[...])
    y = both[:wide] + both[wide:] + dot_nn(weights[0:wide, :], p_lo[...])

    factor = 1.0 / (125.0 * scale)
    for copy_ in loads[1:]:
        copy_.wait()
    chosen = picks[...]
    for s in range(frames):
        for part in range(parts):
            folded = jnp.zeros((coils, LANES), jnp.float32)
            for e in range(5):
                v = y[(s * 5 + e) * coils : (s * 5 + e + 1) * coils, part * LANES : (part + 1) * LANES]
                d = e - 2
                v = jnp.where((x - d >= 0) & (x - d < readout), rolled(v, d), 0.0) if d else v
                folded = folded + v
            folded = folded * factor
            for j in range(rows):
                hit = jnp.where(chosen[s : s + 1, :] == me * rows + j, 1.0, 0.0)
                hit = jnp.max(hit, axis=1, keepdims=True)
                at = place(j, s, part)
                out_ref[at, :] = jnp.where(
                    hit > 0.5, meas[at, :], rolled(folded, -j * readout)[:, :readout]
                )

    def finish(k, carry):
        copy(k + (k >= me).astype(jnp.int32), me).wait_send()
        return carry

    lax.fori_loop(0, n - 1, finish, 0)


def local(estimate, measured, sampled_lines):
    parts, coils, frames, rows, readout = estimate.shape
    n = lax.axis_size("slab")
    assert parts * frames * readout == LANES and frames == 2 and coils % 8 == 0
    assert rows * readout <= LANES and n * rows % 2 == 0 and n * rows >= 16
    flat = (parts * coils * rows * frames, readout)
    deep = n * rows // 2
    chunk = max(d for d in range(1, CHUNK + 1) if deep % d == 0)
    wide = frames * 5 * coils
    tile = frames * LANES
    kinds = 7
    single = chunk == deep
    bf16 = jnp.bfloat16
    any_space = pl.BlockSpec(memory_space=pltpu.HBM)
    stay = functools.partial(pltpu.with_memory_space_constraint, memory_space=pltpu.HBM)
    out = pl.pallas_call(
        functools.partial(kernel, n, (parts, frames, coils, rows, readout)),
        out_shape=jax.ShapeDtypeStruct(flat, jnp.float32),
        in_specs=[any_space] * 3,
        out_specs=pl.BlockSpec(memory_space=pltpu.VMEM),
        scratch_shapes=[
            pltpu.VMEM(flat, jnp.float32),
            pltpu.VMEM(flat, jnp.float32),
            pltpu.VMEM(sampled_lines.shape, jnp.int32),
            pltpu.VMEM((n, rows * coils, LANES), jnp.float32),
            pltpu.VMEM((4 * wide, chunk * LANES), bf16),
            pltpu.VMEM((tile, (chunk + 6) * LANES), bf16),
            pltpu.VMEM((tile, (chunk + 6) * LANES), bf16),
            pltpu.VMEM((2 * wide, 2 * kinds * tile), bf16),
            pltpu.VMEM((2 * kinds * tile, parts * LANES), bf16),
            pltpu.VMEM((2 * kinds * tile, parts * LANES), bf16),
            pltpu.VMEM((1 if single else 3, 2 * wide, tile), jnp.float32),
            pltpu.VMEM((1 if single else 4, 2 * wide, tile), jnp.float32),
            pltpu.SemaphoreType.DMA((n,)),
            pltpu.SemaphoreType.DMA((n,)),
            pltpu.SemaphoreType.DMA((3,)),
        ],
        compiler_params=pltpu.CompilerParams(
            vmem_limit_bytes=40 * 1024 * 1024, collective_id=0, has_side_effects=True
        ),
    )(
        stay(jnp.transpose(estimate, (0, 1, 3, 2, 4)).reshape(flat)),
        stay(jnp.transpose(measured, (0, 1, 3, 2, 4)).reshape(flat)),
        stay(sampled_lines),
    )
    return jnp.transpose(out.reshape(parts, coils, rows, frames, readout), (0, 1, 3, 2, 4))


def solution(mesh):
    placed = (
        P(None, None, "grp", "slab", None),
        P(None, None, "grp", "slab", None),
        P("grp", None),
    )
    return jax.shard_map(
        local,
        mesh=mesh,
        in_specs=placed,
        out_specs=P(None, None, "grp", "slab", None),
        check_vma=False,
    )
```

time: 22.8 us -> 17.5 us (0.77)
  the two profiles are of different devices: /device:TPU:0 before, /device:TPU:13 now
where the time goes in v1:
time: 17.5 us; the launch traced here: 17.3 us
  Pallas kernels  16.7 us (95%)
  local copies, waits for them, and re-layouts  0.62 us (4%)
    pallas_call x1, Pallas kernels, local(): pl.pallas_call(functools.partial(kernel, n, (parts, frames, coils, rows,...  16.7 us
    unnamed x1, local copies, waits for them, and re-layouts  0.62 us

profile of v1, /device:TPU:13, one launch (start us, length us, event | category | flops | bytes accessed | tf_op | source)
XLA Modules:
  0.0 17.3 jit_solution(5116354767350865056)
XLA Ops:
  0.0 16.7 %shard_map.37 = f32[96,32]{1,0:T(8,128)S(1)} custom-call(f32[96,32]{1,0:T(8,128)} %bitcast.10, f32[96,32]{1,0:T(8,128)} %bitcast.11, s32[2,12]{1,0:T(2,128)} %picks_hbm.1), custom_call_target="tpu_custom_call" | custom-call | tf_op jit(solution)/shard_map/pallas_call | solution.py:354
  16.7 0.6 %copy.5 = f32[2,8,2,3,32]{4,2,3,1,0:T(2,128)} copy(f32[2,8,2,3,32]{4,2,3,1,0:T(2,128)S(1)} %bitcast.9) | data formatting | bytes 24576

commit v2 on v1

v2 whole, which is shorter than its diff:
```python
import functools

import jax
import jax.numpy as jnp
from jax import lax
from jax.experimental import pallas as pl
from jax.experimental.pallas import tpu as pltpu
from jax.sharding import PartitionSpec as P

LANES = 128
REACH = 4
SPAN = range(-REACH, REACH + 1)
SMALL = 16


def couplings(frames):
    table = {}
    for s in range(frames):
        for s2 in range(frames):
            for d in range(1 - frames, frames):
                if 0 <= s + d < frames and 0 <= s2 + d < frames:
                    table[s, s2, d] = sum(
                        1
                        for t in range(frames)
                        if 0 <= t + d < frames and abs(s - t) <= 2 and abs(s2 - t) <= 2
                    )
    return {k: v for k, v in table.items() if v}


def halves(x):
    hi = x.astype(jnp.bfloat16)
    return hi, (x - hi.astype(jnp.float32)).astype(jnp.bfloat16)


def dot_nt(a, b):
    return lax.dot_general(a, b, (((1,), (1,)), ((), ())), preferred_element_type=jnp.float32)


def dot_nn(a, b):
    return lax.dot_general(a, b, (((1,), (0,)), ((), ())), preferred_element_type=jnp.float32)


def kernel(
    n, sizes, est_hbm, meas_hbm, picks_hbm, out_ref,
    est, meas, picks, all_ref, even, odd, base, sums, shift, flat, patch, u_hi, u_lo,
    send_sem, recv_sem, in_sem, ready,
):
    parts, frames, coils, rows, readout = sizes
    me = lax.axis_index("slab")
    flip = me >= n - 4
    mine = jnp.where(flip, n - 1 - me, me)
    total = n * rows
    ext = coils * 5
    wide = frames * ext
    bf16 = jnp.bfloat16

    loads = [
        pltpu.make_async_copy(est_hbm, est, in_sem.at[0]),
        pltpu.make_async_copy(meas_hbm, meas, in_sem.at[1]),
        pltpu.make_async_copy(picks_hbm, picks, in_sem.at[2]),
    ]
    for load in loads:
        load.start()

    def greet(j, carry):
        pl.semaphore_signal(pltpu.get_barrier_semaphore(), inc=1, device_id={"slab": j})
        return carry

    lax.fori_loop(me + 1, n, greet, 0)

    def place(line, s, part):
        return pl.ds((part * coils * rows + line) * frames + s, coils, stride=rows * frames)

    loads[0].wait()
    for j in range(rows):
        all_ref[me, j * coils : (j + 1) * coils, :] = jnp.concatenate(
            [est[place(j, s, part), :] for part in range(parts) for s in range(frames)], axis=1
        )
    pl.when(me > 0)(lambda: pl.semaphore_wait(pltpu.get_barrier_semaphore(), me))

    def copy(other, slot):
        return pltpu.make_async_remote_copy(
            src_ref=all_ref.at[slot],
            dst_ref=all_ref.at[slot],
            send_sem=send_sem.at[other],
            recv_sem=recv_sem.at[slot],
            device_id={"slab": other},
        )

    def down(j, carry):
        pl.semaphore_signal(ready.at[me], inc=1, device_id={"slab": j})
        copy(j, me).start()
        return carry

    lax.fori_loop(0, me, down, 0)

    def meet(j, carry):
        pl.semaphore_wait(ready.at[j], 1)
        copy(j, me).start()
        return carry

    first_group = me < 4

    def meet_group(t):
        stop = jnp.where(first_group, 4 * t + 4, me + 1)
        lax.fori_loop(jnp.where(first_group, jnp.maximum(me + 1, 4 * t), me + 1), stop, meet, 0)

    lax.fori_loop(me + 1, jnp.where(first_group, me + 1, n), meet, 0)
    meet_group(0)
    meet_group(1)

    def take(k):
        j = jnp.where(flip, n - 1 - k, k)
        pl.when(j != me)(lambda: copy(j, j).wait_recv())

    lane = lax.broadcasted_iota(jnp.int32, (1, LANES), 1)
    slot = lane // readout
    x = lane % readout
    second = slot >= parts
    turn = jnp.where(slot % parts == 0, 1.0, -1.0)
    nothing = jnp.zeros((coils, LANES), jnp.float32)

    def rolled(v, by):
        by = by % LANES
        return pltpu.roll(v, by, 1) if by else v

    def shifts(v):
        return [
            jnp.where((x + d >= 0) & (x + d < readout), rolled(v, -d), 0.0) if d else v
            for d in range(-2, 3)
        ]

    def line_block(line):
        if isinstance(line, int) and not 0 <= line < total:
            return nothing
        dev, j = line // rows, line % rows
        dev = jnp.where(flip, n - 1 - dev, dev)
        j = jnp.where(flip, rows - 1 - j, j)
        return all_ref[dev, pl.ds(pl.multiple_of(j * coils, coils), coils), :]

    order = [(s, e) for s in range(frames) for e in range(5)]

    def reach_of(line):
        inside = [(line - b >= 0) & (line - b < total) for b in range(-2, 3)]
        if isinstance(line, int):
            return float(sum(inside))
        return sum(jnp.where(v, 1.0, 0.0) for v in inside)

    def at_tile(i):
        start = (i // 2 + 2) * LANES
        return pl.ds(start if isinstance(i, int) else pl.multiple_of(start, LANES), LANES)

    pieces_of = len(order)
    row = lax.broadcasted_iota(jnp.int32, (LANES, LANES), 0)
    part_at = slot % parts
    for b, (s, e) in enumerate(order):
        for k, part in enumerate((part_at, 1 - part_at)):
            from_x = x + e - 2
            target = jnp.where(
                (from_x >= 0) & (from_x < readout), (part * frames + s) * readout + from_x, -1
            )
            one = 1.0 if k == 0 else turn
            shift[:, (k * pieces_of + b) * LANES : (k * pieces_of + b + 1) * LANES] = jnp.where(
                row == target, one, 0.0
            ).astype(bf16)

    def absorb(first, count, energy):
        lines = [line_block(first + k) for k in range(count + 1)]
        for k in range(1, count + 1):
            line = first + k
            if not isinstance(line, int) or line < total:
                energy = energy + reach_of(line) * (lines[k] * lines[k])
        raw = jnp.concatenate(lines, axis=0)
        high = raw.astype(bf16).astype(jnp.float32)
        split = jnp.concatenate([high, raw - high], axis=0).astype(bf16)
        g = dot_nn(split, shift[...])

        def piece(k, w, b):
            top = (w * (count + 1) + k) * coils
            return g[top : top + coils, b * LANES : (b + 1) * LANES]

        for step in range(count):
            i = first + step
            is_even = (step + PARITY) % 2 == 0
            tiles = even if is_even else odd
            at = at_tile(i)
            for w in range(2):
                cells = [
                    jnp.where(second, piece(step + 1, w, b), piece(step, w, b))
                    for b in range(pieces_of)
                ]
                tiles[w * wide : (w + 1) * wide, at] = jnp.concatenate(cells, axis=0).astype(bf16)
                if is_even and (not isinstance(i, int) or 0 <= i < total):
                    both = [
                        jnp.where(second, piece(step + 1, w, b), piece(step, w, b))
                        for b in range(pieces_of, 2 * pieces_of)
                    ]
                    stacked = []
                    for s in range(frames):
                        stacked += [cells[order.index((s, e))] for e in range(5)]
                        stacked += [both[order.index((s, e))] for e in range(5)]
                    base[w * 2 * wide : (w + 1) * 2 * wide, at] = jnp.concatenate(
                        stacked, axis=0
                    ).astype(bf16)
        return energy

    gap = jnp.zeros((LANES - 2 * ext, 1), bf16)

    def columns(at, w, count):
        pad = jnp.broadcast_to(gap, (LANES - 2 * ext, count * LANES))
        pieces = []
        for s in range(frames):
            top = w * 2 * wide + s * 2 * ext
            pieces += [base[top : top + 2 * ext, at], pad]
        return jnp.concatenate(pieces, axis=0)

    def lanes_from(tile, count):
        start = (tile + 2) * LANES
        return pl.ds(start if isinstance(tile, int) else pl.multiple_of(start, LANES), count * LANES)

    def stretch(i, w, count):
        tiles = even if i % 2 == 0 else odd
        return tiles[w * wide : (w + 1) * wide, lanes_from(i // 2, count)]

    def product(rows_hi, rows_lo, cols_hi, cols_lo):
        return dot_nt(
            jnp.concatenate([rows_hi, rows_lo, rows_hi], axis=1),
            jnp.concatenate([cols_hi, cols_hi, cols_lo], axis=1),
        )

    def gram(tile, count, fresh=False):
        at = lanes_from(tile, count)

        def moved(w):
            pieces = []
            for dy in range(REACH + 1):
                tiles = even if dy % 2 == 0 else odd
                pieces.append(tiles[w * wide : (w + 1) * wide, lanes_from(tile + dy // 2, count)])
            return jnp.concatenate(pieces, axis=0)

        g = product(moved(0), moved(1), columns(at, 0, count), columns(at, 1, count))
        sums[...] = g if fresh else sums[...] + g

    def edge(i):
        at = lanes_from(i // 2, 1)

        def picked(w):
            zero = jnp.zeros((wide, LANES), bf16)
            return jnp.concatenate(
                [
                    jnp.where(second, zero, stretch(i, w, 1)),
                    jnp.where(second, zero, stretch(i + 1, w, 1)),
                    jnp.where(second, stretch(i - 1, w, 1), zero),
                    jnp.where(second, stretch(i, w, 1), zero),
                ],
                axis=0,
            )

        return product(picked(0), picked(1), columns(at, 0, 1), columns(at, 1, 1))

    ahead = REACH + 1
    members = [(dy, None) for dy in (*range(ahead), *range(-1, -ahead, -1))]
    for i in (0, total - 2):
        members += [(0, i), (1, i), (-1, i + 1), (0, i + 1)]
    depth = len(members) * wide
    deep = -(-depth // LANES) * LANES
    cells_here = rows * readout

    def patches():
        line_at = mine * rows + slot

        def coefficient(dy, q=None):
            count = jnp.zeros((1, LANES), jnp.float32)
            for b in range(max(-2, -2 - dy), min(2, 2 - dy) + 1):
                if q is not None and 0 <= q - b < total:
                    continue
                count = count + jnp.where((line_at - b >= 0) & (line_at - b < total), 1.0, 0.0)
            return count if q is None else -count

        around = []
        for i in range(rows + 2 * REACH):
            line = mine * rows - REACH + i
            block = line_block(jnp.clip(line, 0, total - 1))
            block = jnp.where((line >= 0) & (line < total), block, 0.0)
            around.append([rolled(block, by * readout) for by in range(LANES // readout)])
        for dy in SPAN:
            for part in range(parts):
                cells = []
                for s in range(frames):
                    v = nothing
                    for j in range(rows):
                        seg = part * frames + s
                        v = jnp.where(slot == j, around[dy + REACH + j][(j - seg) % 4], v)
                    cells.append(shifts(v))
                v = jnp.concatenate([cells[s][e] for s, e in order], axis=0)
                for t, (dy2, q) in enumerate(members):
                    if dy2 == dy:
                        factor = float(couplings(frames)[0, 0, 0]) * coefficient(dy, q)
                        flat[part, t * wide : (t + 1) * wide, :] = factor * v
        for part in range(parts):
            for k in range(0, deep, LANES):
                hi, lo = halves(flat[part, k : k + LANES, :].T[:cells_here])
                at = pl.ds(k, LANES)
                patch[pl.ds(part * cells_here, cells_here), at] = hi
                patch[pl.ds((parts + part) * cells_here, cells_here), at] = lo

    table = couplings(frames)
    unit = float(table[0, 0, 0])

    def mixed(u):
        result = []
        for s2 in range(frames):
            pieces = []
            for s in range(frames):
                whole = None
                for d in range(1 - frames, frames):
                    if (s, s2, d) in table:
                        row = (s + d) * ext
                        term = u[row : row + ext, (s2 + d) * LANES : (s2 + d + 1) * LANES]
                        factor = table[s, s2, d] / unit
                        term = term if factor == 1 else factor * term
                        whole = term if whole is None else whole + term
                pieces.append(whole)
            result.append(jnp.concatenate(pieces, axis=0))
        return result

    def settle(t, cells):
        for s2 in range(frames):
            hi, lo = halves(cells[s2])
            at = pl.ds(s2 * LANES, LANES)
            u_hi[t * wide : (t + 1) * wide, at] = hi
            u_lo[t * wide : (t + 1) * wide, at] = lo

    def mirrored(cells):
        pieces = [[], []]
        for s in range(frames):
            spare = jnp.zeros((LANES - wide, LANES), jnp.float32)
            v = jnp.concatenate([cells[s], spare], axis=0).T
            re, im = v[:ext], v[ext : 2 * ext]
            pieces[0].append(jnp.where(lane < ext, re, -rolled(im, ext)))
            pieces[1].append(jnp.where(lane < ext, rolled(re, -ext), -im))
        return [jnp.concatenate(p, axis=0) for p in pieces]

    for i in (total, total + 1, total + 2):
        tiles = even if i % 2 == 0 else odd
        tiles[:, at_tile(i)] = jnp.zeros((2 * wide, LANES), bf16)
    for part in range(parts):
        flat[part, depth:deep, :] = jnp.zeros((deep - depth, LANES), jnp.float32)
    for ref in (u_hi, u_lo):
        ref[depth:deep, :] = jnp.zeros((deep - depth, frames * LANES), bf16)

    group = 4 * rows
    groups = n // 4
    half = group // 2

    def settle_edge(first, i):
        g = edge(i)
        for k in range(4):
            settle(first + k, mixed(g[k * wide : (k + 1) * wide]))

    energy = nothing
    PARITY = 1
    if n <= SMALL:
        for t in range(groups):
            last = t == groups - 1
            for h in range(2):
                for k in (4 * t + 2 * h, 4 * t + 2 * h + 1):
                    take(k)
                first = group * t + half * h - 1
                PARITY = first % 2
                energy = absorb(first, half + (last and h == 1), energy)
                if last and h == 0:
                    gram((group * t - REACH) // 2, 2)
                    patches()
            lo = max(0, group * t - REACH + (REACH if last else 0))
            hi = group * t + group - (0 if last else REACH)
            if t == 1:
                lo = 0
            if t:
                gram(lo // 2, (hi - lo) // 2, fresh=t == 1)
            if t + 2 < groups:
                meet_group(t + 2)
            if t == 0:
                settle_edge(len(SPAN), 0)
    else:
        lax.fori_loop(2, groups, lambda t, c: (meet_group(t), c)[1], 0)

        def pairs(t):
            for k in range(4):
                take(4 * t + k)

        pairs(0)
        energy = absorb(-1, group, energy)
        gram(0, (group - REACH) // 2, fresh=True)
        settle_edge(len(SPAN), 0)

        def step(t, energy):
            pairs(t)
            energy = absorb(group * t - 1, group, energy)
            gram((group * t - REACH) // 2, group // 2)
            return energy

        energy = lax.fori_loop(1, groups - 1, step, energy)
        pairs(groups - 1)
        first = group * (groups - 1)
        energy = absorb(first - 1, group + 1, energy)
        gram((first - REACH) // 2, (group + REACH) // 2)
        patches()

    settle_edge(len(SPAN) + 4, total - 2)
    for t in range(ahead):
        cells = mixed(sums[t * wide : (t + 1) * wide, :])
        settle(t, cells)
        if t:
            settle(REACH + t, mirrored(cells))

    across = sum(jnp.where((x - d >= 0) & (x - d < readout), 1.0, 0.0) for d in range(-2, 3))
    frame = slot % frames
    for s in range(frames):
        reach = sum(1.0 for t in range(frames) if abs(s - t) <= 2)
        across = jnp.where(frame == s, across * reach, across)
    energy = jnp.sum(energy * across, axis=0, keepdims=True)
    scale = jnp.sum(energy, axis=1, keepdims=True) / (125 * coils) + 1e-06
    factor = 1.0 / (125.0 * scale)

    tall = parts * cells_here
    both = dot_nn(patch[...], u_hi[...])
    y = both[:tall] + both[tall:] + dot_nn(patch[0:tall, :], u_lo[...])

    for load in loads[1:]:
        load.wait()
    chosen = picks[...]
    spare = jnp.zeros((LANES - cells_here, LANES), jnp.float32)
    for s in range(frames):
        turned = []
        for part in range(parts):
            v = y[part * cells_here : (part + 1) * cells_here, s * LANES : (s + 1) * LANES]
            turned.append((jnp.concatenate([v, spare], axis=0) if cells_here < LANES else v).T)
        for part in range(parts):
            folded = nothing
            for e in range(5):
                plain = slice(e * coils, (e + 1) * coils)
                cross = slice(ext + e * coils, ext + (e + 1) * coils)
                if part == 0:
                    v = turned[0][plain] - turned[1][cross]
                else:
                    v = turned[0][cross] + turned[1][plain]
                d = e - 2
                v = jnp.where((x - d >= 0) & (x - d < readout), rolled(v, d), 0.0) if d else v
                folded = folded + v
            folded = folded * factor
            for j in range(rows):
                hit = jnp.where(chosen[s : s + 1, :] == me * rows + j, 1.0, 0.0)
                hit = jnp.max(hit, axis=1, keepdims=True)
                at = place(j, s, part)
                there = jnp.where(
                    flip, rolled(folded, (j + 1 - rows) * readout), rolled(folded, -j * readout)
                )
                out_ref[at, :] = jnp.where(hit > 0.5, meas[at, :], there[:, :readout])

    def finish(k, carry):
        copy(k + (k >= me).astype(jnp.int32), me).wait_send()
        return carry

    lax.fori_loop(0, n - 1, finish, 0)


def local(estimate, measured, sampled_lines):
    parts, coils, frames, rows, readout = estimate.shape
    n = lax.axis_size("slab")
    assert parts * frames * readout == LANES and frames == 2 and coils == 8
    assert rows * readout <= LANES and n % 4 == 0 and n >= 8 and 4 * rows >= 3 * REACH
    flat = (parts * coils * rows * frames, readout)
    total = n * rows
    wide = frames * 5 * coils
    span = (total // 2 + 4) * LANES
    deep = -(-(len(SPAN) + 8) * wide // LANES) * LANES
    cells = rows * readout
    bf16 = jnp.bfloat16
    stay = functools.partial(pltpu.with_memory_space_constraint, memory_space=pltpu.HBM)
    out = pl.pallas_call(
        functools.partial(kernel, n, (parts, frames, coils, rows, readout)),
        out_shape=jax.ShapeDtypeStruct(flat, jnp.float32),
        in_specs=[pl.BlockSpec(memory_space=pltpu.HBM)] * 3,
        out_specs=pl.BlockSpec(memory_space=pltpu.VMEM),
        scratch_shapes=[
            pltpu.VMEM(flat, jnp.float32),
            pltpu.VMEM(flat, jnp.float32),
            pltpu.VMEM(sampled_lines.shape, jnp.int32),
            pltpu.VMEM((n, rows * coils, LANES), jnp.float32),
            pltpu.VMEM((2 * wide, span), bf16),
            pltpu.VMEM((2 * wide, span), bf16),
            pltpu.VMEM((4 * wide, span), bf16),
            pltpu.VMEM(((REACH + 1) * wide, frames * LANES), jnp.float32),
            pltpu.VMEM((LANES, 2 * frames * 5 * LANES), bf16),
            pltpu.VMEM((parts, deep, LANES), jnp.float32),
            pltpu.VMEM((2 * parts * cells, deep), bf16),
            pltpu.VMEM((deep, frames * LANES), bf16),
            pltpu.VMEM((deep, frames * LANES), bf16),
            pltpu.SemaphoreType.DMA((n,)),
            pltpu.SemaphoreType.DMA((n,)),
            pltpu.SemaphoreType.DMA((3,)),
            pltpu.SemaphoreType.REGULAR((n,)),
        ],
        compiler_params=pltpu.CompilerParams(
            vmem_limit_bytes=(40 if n <= SMALL else 56) * 1024 * 1024, collective_id=0, has_side_effects=True
        ),
    )(
        stay(jnp.transpose(estimate, (0, 1, 3, 2, 4)).reshape(flat)),
        stay(jnp.transpose(measured, (0, 1, 3, 2, 4)).reshape(flat)),
        stay(sampled_lines),
    )
    return jnp.transpose(out.reshape(parts, coils, rows, frames, readout), (0, 1, 3, 2, 4))


def solution(mesh):
    placed = (
        P(None, None, "grp", "slab", None),
        P(None, None, "grp", "slab", None),
        P("grp", None),
    )
    return jax.shard_map(
        local,
        mesh=mesh,
        in_specs=placed,
        out_specs=P(None, None, "grp", "slab", None),
        check_vma=False,
    )
```

time: 17.5 us -> 18.2 us (1.040)
  the two profiles are of different devices: /device:TPU:13 before, /device:TPU:17 now
where the time goes in v2:
time: 18.2 us; the launch traced here: 18.1 us
  Pallas kernels  17.5 us (96%)
  local copies, waits for them, and re-layouts  0.62 us (3%)
    pallas_call x1, Pallas kernels, local(): pl.pallas_call(functools.partial(kernel, n, (parts, frames, coils, rows,...  17.5 us
    unnamed x1, local copies, waits for them, and re-layouts  0.62 us

profile of v2, /device:TPU:17, one launch (start us, length us, event | category | flops | bytes accessed | tf_op | source)
XLA Modules:
  0.0 18.1 jit_solution(136109199912086355)
XLA Ops:
  0.0 17.5 %shard_map.37 = f32[96,32]{1,0:T(8,128)S(1)} custom-call(f32[96,32]{1,0:T(8,128)} %bitcast.10, f32[96,32]{1,0:T(8,128)} %bitcast.11, s32[2,12]{1,0:T(2,128)} %picks_hbm.1), custom_call_target="tpu_custom_call" | custom-call | tf_op jit(solution)/shard_map/pallas_call | solution.py:481
  17.5 0.6 %copy.5 = f32[2,8,2,3,32]{4,2,3,1,0:T(2,128)} copy(f32[2,8,2,3,32]{4,2,3,1,0:T(2,128)S(1)} %bitcast.9) | data formatting | bytes 24576

commit v3 on v2

--- a/solution.py
+++ b/solution.py
@@ -361,27 +361,23 @@
     energy = nothing
     PARITY = 1
     if n <= SMALL:
-        for t in range(groups):
-            last = t == groups - 1
-            for h in range(2):
-                for k in (4 * t + 2 * h, 4 * t + 2 * h + 1):
-                    take(k)
-                first = group * t + half * h - 1
-                PARITY = first % 2
-                energy = absorb(first, half + (last and h == 1), energy)
-                if last and h == 0:
-                    gram((group * t - REACH) // 2, 2)
-                    patches()
-            lo = max(0, group * t - REACH + (REACH if last else 0))
-            hi = group * t + group - (0 if last else REACH)
-            if t == 1:
-                lo = 0
-            if t:
-                gram(lo // 2, (hi - lo) // 2, fresh=t == 1)
-            if t + 2 < groups:
-                meet_group(t + 2)
-            if t == 0:
+        for t in range(2, groups - 1):
+            meet_group(t)
+        seen, done = 0, 0
+        for stop in (n // 2, n - 2, n):
+            for k in range(seen, stop):
+                take(k)
+            first = seen * rows - 1
+            PARITY = first % 2
+            energy = absorb(first, (stop - seen) * rows + (stop == n), energy)
+            reached = total if stop == n else (stop * rows - REACH) // 4 * 4
+            gram(done // 2, (reached - done) // 2, fresh=done == 0)
+            if seen == 0:
                 settle_edge(len(SPAN), 0)
+                meet_group(groups - 1)
+            elif stop < n:
+                patches()
+            seen, done = stop, reached
     else:
         lax.fori_loop(2, groups, lambda t, c: (meet_group(t), c)[1], 0)
 

time: 18.2 us -> 17 us (0.934)
  the two profiles are of different devices: /device:TPU:17 before, /device:TPU:27 now
where the time goes in v3:
time: 17 us; the launch traced here: 16.8 us
  Pallas kernels  16.2 us (95%)
  local copies, waits for them, and re-layouts  0.62 us (4%)
    pallas_call x1, Pallas kernels, local(): pl.pallas_call(functools.partial(kernel, n, (parts, frames, coils, rows,...  16.2 us
    unnamed x1, local copies, waits for them, and re-layouts  0.62 us

profile of v3, /device:TPU:27, one launch (start us, length us, event | category | flops | bytes accessed | tf_op | source)
XLA Modules:
  0.0 16.8 jit_solution(11028486053152296615)
XLA Ops:
  0.0 16.2 %shard_map.37 = f32[96,32]{1,0:T(8,128)S(1)} custom-call(f32[96,32]{1,0:T(8,128)} %bitcast.10, f32[96,32]{1,0:T(8,128)} %bitcast.11, s32[2,12]{1,0:T(2,128)} %picks_hbm.1), custom_call_target="tpu_custom_call" | custom-call | tf_op jit(solution)/shard_map/pallas_call | solution.py:477
  16.2 0.6 %copy.5 = f32[2,8,2,3,32]{4,2,3,1,0:T(2,128)} copy(f32[2,8,2,3,32]{4,2,3,1,0:T(2,128)S(1)} %bitcast.9) | data formatting | bytes 24576

commit v4 on v3

--- a/solution.py
+++ b/solution.py
@@ -47,7 +47,7 @@
 ):
     parts, frames, coils, rows, readout = sizes
     me = lax.axis_index("slab")
-    flip = me >= n - 4
+    flip = me >= n // 2
     mine = jnp.where(flip, n - 1 - me, me)
     total = n * rows
     ext = coils * 5
@@ -92,7 +92,8 @@
         copy(j, me).start()
         return carry
 
-    lax.fori_loop(0, me, down, 0)
+    lax.fori_loop(0, jnp.minimum(me, 4), down, 0)
+    lax.fori_loop(4, me, lambda k, c: down(me + 3 - k, c), 0)
 
     def meet(j, carry):
         pl.semaphore_wait(ready.at[j], 1)
@@ -341,6 +342,13 @@
             pieces[1].append(jnp.where(lane < ext, rolled(re, -ext), -im))
         return [jnp.concatenate(p, axis=0) for p in pieces]
 
+    tall = parts * cells_here
+
+    def filtered(first, count):
+        at = pl.ds(first * wide, count * wide)
+        both = dot_nn(patch[:, at], u_hi[at, :])
+        return both[:tall] + both[tall:] + dot_nn(patch[0:tall, at], u_lo[at, :])
+
     for i in (total, total + 1, total + 2):
         tiles = even if i % 2 == 0 else odd
         tiles[:, at_tile(i)] = jnp.zeros((2 * wide, LANES), bf16)
@@ -359,6 +367,7 @@
             settle(first + k, mixed(g[k * wide : (k + 1) * wide]))
 
     energy = nothing
+    early = []
     PARITY = 1
     if n <= SMALL:
         for t in range(2, groups - 1):
@@ -370,13 +379,15 @@
             first = seen * rows - 1
             PARITY = first % 2
             energy = absorb(first, (stop - seen) * rows + (stop == n), energy)
+            if seen == 0:
+                meet_group(groups - 1)
             reached = total if stop == n else (stop * rows - REACH) // 4 * 4
             gram(done // 2, (reached - done) // 2, fresh=done == 0)
             if seen == 0:
                 settle_edge(len(SPAN), 0)
-                meet_group(groups - 1)
             elif stop < n:
                 patches()
+                early.append(filtered(len(SPAN), 4))
             seen, done = stop, reached
     else:
         lax.fori_loop(2, groups, lambda t, c: (meet_group(t), c)[1], 0)
@@ -419,9 +430,9 @@
     scale = jnp.sum(energy, axis=1, keepdims=True) / (125 * coils) + 1e-06
     factor = 1.0 / (125.0 * scale)
 
-    tall = parts * cells_here
-    both = dot_nn(patch[...], u_hi[...])
-    y = both[:tall] + both[tall:] + dot_nn(patch[0:tall, :], u_lo[...])
+    y = filtered(0, len(SPAN)) + filtered(len(SPAN) + 4, 4)
+    for part in early or [filtered(len(SPAN), 4)]:
+        y = y + part
 
     for load in loads[1:]:
         load.wait()

time: 17 us -> 15.6 us (0.918)
  the two profiles are of different devices: /device:TPU:27 before, /device:TPU:17 now
where the time goes in v4:
time: 15.6 us; the launch traced here: 15.4 us
  Pallas kernels  14.8 us (95%)
  local copies, waits for them, and re-layouts  0.62 us (4%)
    pallas_call x1, Pallas kernels, local(): pl.pallas_call(functools.partial(kernel, n, (parts, frames, coils, rows,...  14.8 us
    unnamed x1, local copies, waits for them, and re-layouts  0.62 us

profile of v4, /device:TPU:17, one launch (start us, length us, event | category | flops | bytes accessed | tf_op | source)
XLA Modules:
  0.0 15.4 jit_solution(4466939554367974904)
XLA Ops:
  0.0 14.8 %shard_map.37 = f32[96,32]{1,0:T(8,128)S(1)} custom-call(f32[96,32]{1,0:T(8,128)} %bitcast.10, f32[96,32]{1,0:T(8,128)} %bitcast.11, s32[2,12]{1,0:T(2,128)} %picks_hbm.1), custom_call_target="tpu_custom_call" | custom-call | tf_op jit(solution)/shard_map/pallas_call | solution.py:488
  14.8 0.6 %copy.5 = f32[2,8,2,3,32]{4,2,3,1,0:T(2,128)} copy(f32[2,8,2,3,32]{4,2,3,1,0:T(2,128)S(1)} %bitcast.9) | data formatting | bytes 24576

commit v5 on v4

--- a/solution.py
+++ b/solution.py
@@ -82,7 +82,7 @@
         return pltpu.make_async_remote_copy(
             src_ref=all_ref.at[slot],
             dst_ref=all_ref.at[slot],
-            send_sem=send_sem.at[other],
+            send_sem=send_sem,
             recv_sem=recv_sem.at[slot],
             device_id={"slab": other},
         )
@@ -92,8 +92,12 @@
         copy(j, me).start()
         return carry
 
+    def down_group(t, carry):
+        g = me // 4 - t
+        return lax.fori_loop(4 * g, jnp.minimum(4 * g + 4, me), down, carry)
+
     lax.fori_loop(0, jnp.minimum(me, 4), down, 0)
-    lax.fori_loop(4, me, lambda k, c: down(me + 3 - k, c), 0)
+    lax.fori_loop(0, me // 4, down_group, 0)
 
     def meet(j, carry):
         pl.semaphore_wait(ready.at[j], 1)
@@ -366,6 +370,8 @@
         for k in range(4):
             settle(first + k, mixed(g[k * wide : (k + 1) * wide]))
 
+    for load in loads[1:]:
+        load.wait()
     energy = nothing
     early = []
     PARITY = 1
@@ -373,22 +379,24 @@
         for t in range(2, groups - 1):
             meet_group(t)
         seen, done = 0, 0
-        for stop in (n // 2, n - 2, n):
+        for stop in (n // 4, n // 2, n - 2, n):
             for k in range(seen, stop):
                 take(k)
             first = seen * rows - 1
             PARITY = first % 2
             energy = absorb(first, (stop - seen) * rows + (stop == n), energy)
-            if seen == 0:
+            if stop == n // 2:
                 meet_group(groups - 1)
-            reached = total if stop == n else (stop * rows - REACH) // 4 * 4
-            gram(done // 2, (reached - done) // 2, fresh=done == 0)
+            if stop in (n // 2, n - 2, n):
+                reached = total if stop == n else (stop * rows - REACH) // 4 * 4
+                gram(done // 2, (reached - done) // 2, fresh=done == 0)
+                done = reached
             if seen == 0:
                 settle_edge(len(SPAN), 0)
-            elif stop < n:
+            if stop == n - 2:
                 patches()
                 early.append(filtered(len(SPAN), 4))
-            seen, done = stop, reached
+            seen = stop
     else:
         lax.fori_loop(2, groups, lambda t, c: (meet_group(t), c)[1], 0)
 
@@ -434,8 +442,6 @@
     for part in early or [filtered(len(SPAN), 4)]:
         y = y + part
 
-    for load in loads[1:]:
-        load.wait()
     chosen = picks[...]
     spare = jnp.zeros((LANES - cells_here, LANES), jnp.float32)
     for s in range(frames):
@@ -465,11 +471,14 @@
                 )
                 out_ref[at, :] = jnp.where(hit > 0.5, meas[at, :], there[:, :readout])
 
-    def finish(k, carry):
-        copy(k + (k >= me).astype(jnp.int32), me).wait_send()
-        return carry
-
-    lax.fori_loop(0, n - 1, finish, 0)
+    others = all_ref.at[pl.ds(0, n - 1)]
+    pltpu.make_async_remote_copy(
+        src_ref=others,
+        dst_ref=others,
+        send_sem=send_sem,
+        recv_sem=recv_sem.at[me],
+        device_id={"slab": lax.rem(me + 1, n)},
+    ).wait_send()
 
 
 def local(estimate, measured, sampled_lines):
@@ -504,7 +513,7 @@
             pltpu.VMEM((2 * parts * cells, deep), bf16),
             pltpu.VMEM((deep, frames * LANES), bf16),
             pltpu.VMEM((deep, frames * LANES), bf16),
-            pltpu.SemaphoreType.DMA((n,)),
+            pltpu.SemaphoreType.DMA,
             pltpu.SemaphoreType.DMA((n,)),
             pltpu.SemaphoreType.DMA((3,)),
             pltpu.SemaphoreType.REGULAR((n,)),

time: 15.6 us -> 14.9 us (0.955)
  Pallas kernels: 14.8 us -> 14 us
    pallas_call x1, Pallas kernels: 14.8 us -> 14 us  [local(): pl.pallas_call(functools.partial(kernel, n, (parts, frames, coils, rows,...]
where the time goes in v5:
time: 14.9 us; the launch traced here: 14.6 us
  Pallas kernels  14 us (94%)
  local copies, waits for them, and re-layouts  0.62 us (4%)
    pallas_call x1, Pallas kernels, local(): pl.pallas_call(functools.partial(kernel, n, (parts, frames, coils, rows,...  14 us
    unnamed x1, local copies, waits for them, and re-layouts  0.62 us

profile of v5, /device:TPU:17, one launch (start us, length us, event | category | flops | bytes accessed | tf_op | source)
XLA Modules:
  0.0 14.6 jit_solution(509680374921274420)
XLA Ops:
  0.0 14.0 %shard_map.37 = f32[96,32]{1,0:T(8,128)S(1)} custom-call(f32[96,32]{1,0:T(8,128)} %bitcast.10, f32[96,32]{1,0:T(8,128)} %bitcast.11, s32[2,12]{1,0:T(2,128)} %picks_hbm.1), custom_call_target="tpu_custom_call" | custom-call | tf_op jit(solution)/shard_map/pallas_call | solution.py:497
  14.0 0.6 %copy.5 = f32[2,8,2,3,32]{4,2,3,1,0:T(2,128)} copy(f32[2,8,2,3,32]{4,2,3,1,0:T(2,128)S(1)} %bitcast.9) | data formatting | bytes 24576

commit v6 on v5

--- a/solution.py
+++ b/solution.py
@@ -382,11 +382,11 @@
         for stop in (n // 4, n // 2, n - 2, n):
             for k in range(seen, stop):
                 take(k)
+            if stop == n // 2:
+                meet_group(groups - 1)
             first = seen * rows - 1
             PARITY = first % 2
             energy = absorb(first, (stop - seen) * rows + (stop == n), energy)
-            if stop == n // 2:
-                meet_group(groups - 1)
             if stop in (n // 2, n - 2, n):
                 reached = total if stop == n else (stop * rows - REACH) // 4 * 4
                 gram(done // 2, (reached - done) // 2, fresh=done == 0)
@@ -422,12 +422,12 @@
         gram((first - REACH) // 2, (group + REACH) // 2)
         patches()
 
-    settle_edge(len(SPAN) + 4, total - 2)
-    for t in range(ahead):
+    for t in (*range(1, ahead), 0):
         cells = mixed(sums[t * wide : (t + 1) * wide, :])
         settle(t, cells)
         if t:
             settle(REACH + t, mirrored(cells))
+    settle_edge(len(SPAN) + 4, total - 2)
 
     across = sum(jnp.where((x - d >= 0) & (x - d < readout), 1.0, 0.0) for d in range(-2, 3))
     frame = slot % frames

time: 14.9 us -> 14.9 us (level)
  the two profiles are of different devices: /device:TPU:17 before, /device:TPU:25 now
where the time goes in v6:
time: 14.9 us; the launch traced here: 14.8 us
  Pallas kernels  14.1 us (95%)
  local copies, waits for them, and re-layouts  0.62 us (4%)
    pallas_call x1, Pallas kernels, local(): pl.pallas_call(functools.partial(kernel, n, (parts, frames, coils, rows,...  14.1 us
    unnamed x1, local copies, waits for them, and re-layouts  0.62 us

profile of v6, /device:TPU:25, one launch (start us, length us, event | category | flops | bytes accessed | tf_op | source)
XLA Modules:
  0.0 14.8 jit_solution(8296463424862090328)
XLA Ops:
  0.0 14.1 %shard_map.37 = f32[96,32]{1,0:T(8,128)S(1)} custom-call(f32[96,32]{1,0:T(8,128)} %bitcast.10, f32[96,32]{1,0:T(8,128)} %bitcast.11, s32[2,12]{1,0:T(2,128)} %picks_hbm.1), custom_call_target="tpu_custom_call" | custom-call | tf_op jit(solution)/shard_map/pallas_call | solution.py:497
  14.1 0.6 %copy.5 = f32[2,8,2,3,32]{4,2,3,1,0:T(2,128)} copy(f32[2,8,2,3,32]{4,2,3,1,0:T(2,128)S(1)} %bitcast.9) | data formatting | bytes 24576

commit v7 on v6

--- a/solution.py
+++ b/solution.py
@@ -372,6 +372,12 @@
 
     for load in loads[1:]:
         load.wait()
+    chosen = picks[...]
+    hits = {}
+    for s in range(frames):
+        for j in range(rows):
+            hit = jnp.where(chosen[s : s + 1, :] == me * rows + j, 1.0, 0.0)
+            hits[s, j] = jnp.max(hit, axis=1, keepdims=True)
     energy = nothing
     early = []
     PARITY = 1
@@ -382,11 +388,11 @@
         for stop in (n // 4, n // 2, n - 2, n):
             for k in range(seen, stop):
                 take(k)
-            if stop == n // 2:
-                meet_group(groups - 1)
             first = seen * rows - 1
             PARITY = first % 2
             energy = absorb(first, (stop - seen) * rows + (stop == n), energy)
+            if stop == n // 2:
+                meet_group(groups - 1)
             if stop in (n // 2, n - 2, n):
                 reached = total if stop == n else (stop * rows - REACH) // 4 * 4
                 gram(done // 2, (reached - done) // 2, fresh=done == 0)
@@ -442,7 +448,6 @@
     for part in early or [filtered(len(SPAN), 4)]:
         y = y + part
 
-    chosen = picks[...]
     spare = jnp.zeros((LANES - cells_here, LANES), jnp.float32)
     for s in range(frames):
         turned = []
@@ -463,8 +468,7 @@
                 folded = folded + v
             folded = folded * factor
             for j in range(rows):
-                hit = jnp.where(chosen[s : s + 1, :] == me * rows + j, 1.0, 0.0)
-                hit = jnp.max(hit, axis=1, keepdims=True)
+                hit = hits[s, j]
                 at = place(j, s, part)
                 there = jnp.where(
                     flip, rolled(folded, (j + 1 - rows) * readout), rolled(folded, -j * readout)

time: 14.9 us -> 14.9 us (level)
  the two profiles are of different devices: /device:TPU:25 before, /device:TPU:17 now
where the time goes in v7:
time: 14.9 us; the launch traced here: 14.6 us
  Pallas kernels  14 us (94%)
  local copies, waits for them, and re-layouts  0.62 us (4%)
    pallas_call x1, Pallas kernels, local(): pl.pallas_call(functools.partial(kernel, n, (parts, frames, coils, rows,...  14 us
    unnamed x1, local copies, waits for them, and re-layouts  0.62 us

profile of v7, /device:TPU:17, one launch (start us, length us, event | category | flops | bytes accessed | tf_op | source)
XLA Modules:
  0.0 14.6 jit_solution(14507579119109240223)
XLA Ops:
  0.0 14.0 %shard_map.37 = f32[96,32]{1,0:T(8,128)S(1)} custom-call(f32[96,32]{1,0:T(8,128)} %bitcast.10, f32[96,32]{1,0:T(8,128)} %bitcast.11, s32[2,12]{1,0:T(2,128)} %picks_hbm.1), custom_call_target="tpu_custom_call" | custom-call | tf_op jit(solution)/shard_map/pallas_call | solution.py:501
  14.0 0.6 %copy.5 = f32[2,8,2,3,32]{4,2,3,1,0:T(2,128)} copy(f32[2,8,2,3,32]{4,2,3,1,0:T(2,128)S(1)} %bitcast.9) | data formatting | bytes 24576
